TPU v7x, 32 devices: a whole 2x2x4 slice. The times are simulated.
32 devices in a mesh: rep: 8 (over z, x), shard: 4 (over y, core).
Axes of the slice: x: 2, y: 2, z: 4, core: 2. Of those that a mesh axis runs over, the one named last changes fastest.
Arguments:
- latent_tokens: bfloat16 [256, 256, 384], P(('rep', 'shard')), may hold values from -6 to 6
- cond: bfloat16 [256, 384], P(('rep', 'shard')), may hold values from -6 to 6
- w_ada: bfloat16 [384, 2304], P('shard'), may hold values from -0.3125 to 0.3125
- b_ada: bfloat16 [2304], P('shard'), may hold values from -3 to 3
- w_qkv: bfloat16 [384, 1152], P('shard'), may hold values from -0.3125 to 0.3125
- b_qv: bfloat16 [768], P('shard'), may hold values from -3 to 3
- w_o: bfloat16 [384, 384], P('shard'), may hold values from -0.875 to 0.875
- b_o: bfloat16 [384], P('shard'), may hold values from -3 to 3
- w_1: bfloat16 [384, 1536], P('shard'), may hold values from -0.3125 to 0.3125
- b_1: bfloat16 [1536], P('shard'), may hold values from -3 to 3
- w_2: bfloat16 [1536, 384], P('shard'), may hold values from -0.15625 to 0.15625
- b_2: bfloat16 [384], P('shard'), may hold values from -3 to 3
- grad_out: bfloat16 [256, 256, 384], P(('rep', 'shard')), may hold values from -6 to 6
Outputs:
- block_out: bfloat16 [256, 256, 384], P(('rep', 'shard'))
- grad_tokens: float32 [256, 256, 384], P(('rep', 'shard'))
- grad_cond: float32 [256, 384], P(('rep', 'shard'))
- grad_w_ada: float32 [384, 2304], P('shard')
- grad_b_ada: float32 [2304], P('shard')
- grad_w_qkv: float32 [384, 1152], P('shard')
- grad_b_qv: float32 [768], P('shard')
- grad_w_o: float32 [384, 384], P('shard')
- grad_b_o: float32 [384], P('shard')
- grad_w_1: float32 [384, 1536], P('shard')
- grad_b_1: float32 [1536], P('shard')
- grad_w_2: float32 [1536, 384], P('shard')
- grad_b_2: float32 [384], P('shard')
All inputs are finite; a program needn't handle non-finite values.
Results may differ from a plain program's by a relative error of at most 0.019.
The roundings to bfloat16 on the way count: a program that leaves them out, or rounds other values in their place, can miss the bound.
Values may be sent and summed in bfloat16 or wider, within the bound.
No kernel may reach another device: no remote copies, remote signals or barrier semaphores. Data moves between devices by JAX's collectives and lax.ppermute only.
A program may use at most 128 MiB of HBM per device.

v0:
```python
import math
import jax
import jax.numpy as jnp
from jax import lax
from jax.sharding import PartitionSpec as P

HEADS = 6


def layer_norm(value):
    centred = value - jnp.mean(value, axis=-1, keepdims=True)
    factor = lax.rsqrt(jnp.mean(centred * centred, axis=-1, keepdims=True) + 1e-06)
    return (centred * factor, factor)


def norm_back(normed, factor, grad_normed):
    inner = jnp.mean(grad_normed, axis=-1, keepdims=True)
    along = jnp.mean(grad_normed * normed, axis=-1, keepdims=True)
    return factor * (grad_normed - inner - normed * along)


def project(left, right):
    return jnp.einsum("lsd,de->lse", left, right, preferred_element_type=jnp.float32)


def weight_grad(left, right):
    return jnp.einsum("lsd,lse->de", left, right, preferred_element_type=jnp.float32)


def attend(items):
    query, key, value = items
    scores = jnp.einsum("lqhd,lkhd->lhqk", query, key, preferred_element_type=jnp.float32) * 0.125
    top = jnp.max(scores, axis=-1, keepdims=True)
    expo = jnp.exp(scores - top)
    total = jnp.sum(expo, axis=-1, keepdims=True)
    probs = (expo / total).astype(jnp.bfloat16)
    attended = jnp.einsum("lhqk,lkhd->lqhd", probs, value, preferred_element_type=jnp.float32)
    return (attended.astype(jnp.bfloat16), top + jnp.log(total))


def attend_back(items):
    query, key, value, logsum, grad_att = items
    scores = jnp.einsum("lqhd,lkhd->lhqk", query, key, preferred_element_type=jnp.float32) * 0.125
    probs = jnp.exp(scores - logsum)
    rounded = probs.astype(jnp.bfloat16)
    grad_value = jnp.einsum(
        "lhqk,lqhd->lkhd", rounded, grad_att, preferred_element_type=jnp.float32
    )
    grad_probs = jnp.einsum("lqhd,lkhd->lhqk", grad_att, value, preferred_element_type=jnp.float32)
    row_total = jnp.sum(probs * grad_probs, axis=-1, keepdims=True)
    grad_scores = (probs * (grad_probs - row_total)).astype(jnp.bfloat16)
    grad_query = (
        jnp.einsum("lhqk,lkhd->lqhd", grad_scores, key, preferred_element_type=jnp.float32) * 0.125
    )
    grad_key = (
        jnp.einsum("lhqk,lqhd->lkhd", grad_scores, query, preferred_element_type=jnp.float32)
        * 0.125
    )
    return (
        grad_query.astype(jnp.bfloat16),
        grad_key.astype(jnp.bfloat16),
        grad_value.astype(jnp.bfloat16),
    )


def on_device(
    latent_tokens, cond, w_ada, b_ada, w_qkv, b_qv, w_o, b_o, w_1, b_1, w_2, b_2, grad_out
):
    count, length, width = latent_tokens.shape
    head_size = width // HEADS
    per_block = math.gcd(count, max(1, 512 // length))
    blocks = count // per_block
    whole = (
        lax.all_gather(w_ada, "shard", axis=0, tiled=True),
        lax.all_gather(b_ada, "shard", axis=0, tiled=True),
        lax.all_gather(w_qkv, "shard", axis=0, tiled=True),
        lax.all_gather(b_qv, "shard", axis=0, tiled=True),
        lax.all_gather(w_o, "shard", axis=0, tiled=True),
        lax.all_gather(b_o, "shard", axis=0, tiled=True),
        lax.all_gather(w_1, "shard", axis=0, tiled=True),
        lax.all_gather(b_1, "shard", axis=0, tiled=True),
        lax.all_gather(w_2, "shard", axis=0, tiled=True),
        lax.all_gather(b_2, "shard", axis=0, tiled=True),
    )
    f_ada, f_bada, f_qkv, f_bqv, f_wo, f_bo, f_w1, f_b1, f_w2, f_b2 = whole
    tokens = latent_tokens.astype(jnp.float32)
    condition = cond.astype(jnp.float32)
    cs = jax.nn.silu(condition).astype(jnp.bfloat16)
    ada = jnp.dot(cs, f_ada, preferred_element_type=jnp.float32) + f_bada.astype(jnp.float32)
    shift1, scale1, gate1, shift2, scale2, gate2 = jnp.split(ada, 6, axis=-1)
    n1, rstd1 = layer_norm(tokens)
    m1 = (n1 * (1.0 + scale1[:, None]) + shift1[:, None]).astype(jnp.bfloat16)
    qkv = project(m1, f_qkv)
    bias_qv = f_bqv.astype(jnp.float32)
    query = (qkv[..., :width] + bias_qv[:width]).astype(jnp.bfloat16)
    key = qkv[..., width : 2 * width].astype(jnp.bfloat16)
    value = (qkv[..., 2 * width :] + bias_qv[width:]).astype(jnp.bfloat16)
    shape_blocks = (blocks, per_block, length, HEADS, head_size)
    q_blocks = query.reshape(shape_blocks)
    k_blocks = key.reshape(shape_blocks)
    v_blocks = value.reshape(shape_blocks)
    att_blocks, logsum = lax.map(attend, (q_blocks, k_blocks, v_blocks))
    attended = att_blocks.reshape(count, length, width)
    branch = project(attended, f_wo) + f_bo.astype(jnp.float32)
    x1 = tokens + gate1[:, None] * branch
    n2, rstd2 = layer_norm(x1)
    m2 = (n2 * (1.0 + scale2[:, None]) + shift2[:, None]).astype(jnp.bfloat16)
    hidden = project(m2, f_w1) + f_b1.astype(jnp.float32)
    gelu_out, gelu_vjp = jax.vjp(lambda t: jax.nn.gelu(t, approximate=True), hidden)
    gelu_low = gelu_out.astype(jnp.bfloat16)
    ffn = project(gelu_low, f_w2) + f_b2.astype(jnp.float32)
    block_out = (x1 + gate2[:, None] * ffn).astype(jnp.bfloat16)
    again = (
        lax.all_gather(w_ada, "shard", axis=0, tiled=True),
        lax.all_gather(w_qkv, "shard", axis=0, tiled=True),
        lax.all_gather(w_o, "shard", axis=0, tiled=True),
        lax.all_gather(w_1, "shard", axis=0, tiled=True),
        lax.all_gather(w_2, "shard", axis=0, tiled=True),
    )
    g_ada, g_qkv, g_wo, g_w1, g_w2 = again
    cotangent = grad_out.astype(jnp.float32)
    grad_ffn = (cotangent * gate2[:, None]).astype(jnp.bfloat16)
    d_gate2 = jnp.sum(cotangent * ffn, axis=1)
    gw_2 = weight_grad(gelu_low, grad_ffn)
    gb_2 = jnp.sum(grad_ffn.astype(jnp.float32), axis=(0, 1))
    grad_gelu = jnp.einsum("lse,de->lsd", grad_ffn, g_w2, preferred_element_type=jnp.float32)
    grad_hidden = gelu_vjp(grad_gelu)[0].astype(jnp.bfloat16)
    gw_1 = weight_grad(m2, grad_hidden)
    gb_1 = jnp.sum(grad_hidden.astype(jnp.float32), axis=(0, 1))
    grad_m2 = jnp.einsum("lse,de->lsd", grad_hidden, g_w1, preferred_element_type=jnp.float32)
    d_scale2 = jnp.sum(grad_m2 * n2, axis=1)
    d_shift2 = jnp.sum(grad_m2, axis=1)
    grad_x1 = cotangent + norm_back(n2, rstd2, grad_m2 * (1.0 + scale2[:, None]))
    grad_branch = (grad_x1 * gate1[:, None]).astype(jnp.bfloat16)
    d_gate1 = jnp.sum(grad_x1 * branch, axis=1)
    gw_o = weight_grad(attended, grad_branch)
    gb_o = jnp.sum(grad_branch.astype(jnp.float32), axis=(0, 1))
    grad_att = jnp.einsum(
        "lse,de->lsd", grad_branch, g_wo, preferred_element_type=jnp.float32
    ).astype(jnp.bfloat16)
    dq, dk, dv = lax.map(
        attend_back, (q_blocks, k_blocks, v_blocks, logsum, grad_att.reshape(shape_blocks))
    )
    grad_qkv = jnp.concatenate(
        [
            dq.reshape(count, length, width),
            dk.reshape(count, length, width),
            dv.reshape(count, length, width),
        ],
        axis=-1,
    )
    gw_qkv = weight_grad(m1, grad_qkv)
    column_sums = jnp.sum(grad_qkv.astype(jnp.float32), axis=(0, 1))
    gb_qv = jnp.concatenate([column_sums[:width], column_sums[2 * width :]])
    grad_m1 = jnp.einsum("lse,de->lsd", grad_qkv, g_qkv, preferred_element_type=jnp.float32)
    d_scale1 = jnp.sum(grad_m1 * n1, axis=1)
    d_shift1 = jnp.sum(grad_m1, axis=1)
    grad_tokens = grad_x1 + norm_back(n1, rstd1, grad_m1 * (1.0 + scale1[:, None]))
    grad_ada = jnp.concatenate(
        [d_shift1, d_scale1, d_gate1, d_shift2, d_scale2, d_gate2], axis=-1
    ).astype(jnp.bfloat16)
    gw_ada = jnp.dot(cs.T, grad_ada, preferred_element_type=jnp.float32)
    gb_ada = jnp.sum(grad_ada.astype(jnp.float32), axis=0)
    grad_cs = jnp.dot(grad_ada, g_ada.T, preferred_element_type=jnp.float32)
    silu_grad = jax.vjp(jax.nn.silu, condition)[1](grad_cs)[0]
    partial_value = (
        lax.psum_scatter(
            gw_ada.astype(jnp.bfloat16), "shard", scatter_dimension=0, tiled=True
        ).astype(jnp.float32),
        lax.psum_scatter(
            gb_ada.astype(jnp.bfloat16), "shard", scatter_dimension=0, tiled=True
        ).astype(jnp.float32),
        lax.psum_scatter(
            gw_qkv.astype(jnp.bfloat16), "shard", scatter_dimension=0, tiled=True
        ).astype(jnp.float32),
        lax.psum_scatter(
            gb_qv.astype(jnp.bfloat16), "shard", scatter_dimension=0, tiled=True
        ).astype(jnp.float32),
        lax.psum_scatter(
            gw_o.astype(jnp.bfloat16), "shard", scatter_dimension=0, tiled=True
        ).astype(jnp.float32),
        lax.psum_scatter(
            gb_o.astype(jnp.bfloat16), "shard", scatter_dimension=0, tiled=True
        ).astype(jnp.float32),
        lax.psum_scatter(
            gw_1.astype(jnp.bfloat16), "shard", scatter_dimension=0, tiled=True
        ).astype(jnp.float32),
        lax.psum_scatter(
            gb_1.astype(jnp.bfloat16), "shard", scatter_dimension=0, tiled=True
        ).astype(jnp.float32),
        lax.psum_scatter(
            gw_2.astype(jnp.bfloat16), "shard", scatter_dimension=0, tiled=True
        ).astype(jnp.float32),
        lax.psum_scatter(
            gb_2.astype(jnp.bfloat16), "shard", scatter_dimension=0, tiled=True
        ).astype(jnp.float32),
    )
    summed = (
        lax.psum(partial_value[0].astype(jnp.bfloat16), "rep").astype(jnp.float32),
        lax.psum(partial_value[1].astype(jnp.bfloat16), "rep").astype(jnp.float32),
        lax.psum(partial_value[2].astype(jnp.bfloat16), "rep").astype(jnp.float32),
        lax.psum(partial_value[3].astype(jnp.bfloat16), "rep").astype(jnp.float32),
        lax.psum(partial_value[4].astype(jnp.bfloat16), "rep").astype(jnp.float32),
        lax.psum(partial_value[5].astype(jnp.bfloat16), "rep").astype(jnp.float32),
        lax.psum(partial_value[6].astype(jnp.bfloat16), "rep").astype(jnp.float32),
        lax.psum(partial_value[7].astype(jnp.bfloat16), "rep").astype(jnp.float32),
        lax.psum(partial_value[8].astype(jnp.bfloat16), "rep").astype(jnp.float32),
        lax.psum(partial_value[9].astype(jnp.bfloat16), "rep").astype(jnp.float32),
    )
    return (
        block_out,
        grad_tokens,
        silu_grad,
        summed[0],
        summed[1],
        summed[2],
        summed[3],
        summed[4],
        summed[5],
        summed[6],
        summed[7],
        summed[8],
        summed[9],
    )


def solution(mesh):
    in_specs = (
        P(("rep", "shard"), None, None),
        P(("rep", "shard"), None),
        P("shard", None),
        P("shard"),
        P("shard", None),
        P("shard"),
        P("shard", None),
        P("shard"),
        P("shard", None),
        P("shard"),
        P("shard", None),
        P("shard"),
        P(("rep", "shard"), None, None),
    )
    out_specs = (
        P(("rep", "shard"), None, None),
        P(("rep", "shard"), None, None),
        P(("rep", "shard"), None),
        P("shard", None),
        P("shard"),
        P("shard", None),
        P("shard"),
        P("shard", None),
        P("shard"),
        P("shard", None),
        P("shard"),
        P("shard", None),
        P("shard"),
    )
    return jax.shard_map(
        on_device, mesh=mesh, in_specs=in_specs, out_specs=out_specs, check_vma=False
    )
```

profile of v0, /device:TPU:0, one launch (start us, length us, event | category | flops | bytes accessed | tf_op | source)
XLA Modules:
  0.0 425.0 jit_solution(18000375624998559178)
XLA Ops:
  13.5 6.1 %all-gather = bf16[4,1,384]{2,1,0:T(2,128)(2,1)S(1)} all-gather(bf16[1,1,384]{2,1,0:T(2,128)(2,1)S(1)} %reshape.148), channel_id=1, replica_groups=mesh['rep'=8,'shard'=4] {'shard'}, dimensions={0}, use_global_device_ids=true | all-gather | bytes 3840 | tf_op jit(solution)/shard_map/all_gather | solution.py:81
  23.6 12.3 %all-reduce.12 = (bf16[2304]{0:T(1024)(128)(2,1)S(1)}, bf16[768]{0:T(1024)(128)(2,1)S(1)}, bf16[384]{0:T(512)(128)(2,1)S(1)}, bf16[384]{0:T(512)(128)(2,1)S(1)}) all-reduce(bf16[2304]{0:T(1024)(128)(2,1)S(1)} %dynamic-update-slice, bf16[768]{0:T(1024)(128)(2,1)S(1)} %dynamic-update-slice.1, ...), channel_id=1, replica_groups=mesh['rep'=8,'shard'=4] {'shard'}, use_global_device_ids=true, to_apply=%add | all-reduce | flops 3840 | bytes 15360
  39.2 5.9 %all_gather.39 = bf16[384,384]{1,0:T(8,128)(2,1)S(1)} all-gather(bf16[96,384]{1,0:T(8,128)(2,1)S(1)} %copy-done.16), channel_id=1, replica_groups=mesh['rep'=8,'shard'=4] {'shard'}, dimensions={0}, use_global_device_ids=true | all-gather | bytes 368640 | tf_op jit(solution)/shard_map/all_gather | solution.py:78
  45.1 11.3 %all_gather.37 = bf16[384,1152]{1,0:T(8,128)(2,1)S(1)} all-gather(bf16[96,1152]{1,0:T(8,128)(2,1)S(1)} %copy-done.15), channel_id=1, replica_groups=mesh['rep'=8,'shard'=4] {'shard'}, dimensions={0}, use_global_device_ids=true | all-gather | bytes 1105920 | tf_op jit(solution)/shard_map/all_gather | solution.py:76
  59.2 3.0 fusion.98
  67.6 2.6 copy.80
  70.2 2.6 copy.78
  74.2 18.9 %while.26 = (s32[]{:T(128)}, bf16[4,2,256,6,64]{2,4,3,1,0:T(8,128)(2,1)}, f32[4,2,6,256,1]{3,2,1,4,0:T(8,128)S(1)}, bf16[4,2,256,6,64]{2,4,3,1,0:T(8,128)(2,1)},...) while((s32[]{:T(128)}, ...), condition=%wide.region_5.6_spmd, body=%wide.region_2.5_spmd.sunk | while | flops 208598016 | bytes 11122777 | solution.py:102
  81.1 2.5 fusion.152
  85.8 2.5 fusion.152
  93.1 4.6 %fusion.115 = (f32[8,256]{1,0:T(8,128)S(1)}, f32[8,256,384]{2,1,0:T(8,128)S(1)}, f32[8,256,384]{2,1,0:T(8,128)}) fusion(f32[384]{0:T(512)S(1)} %convert_element_type.177, f32[8,384]{1,0:T(8,128)S(1)} %get-tuple-element.197, bf16[8,256,384]{2,1,0:T(8,128)(2,1)S(1)} %copy-done, bf16[8,256,384]{1,2,0:T(8,128)(2,1)} %bitcast.178, ...), kind=kOutput, calls=%fused_computation.164 | convolution fusion | flops 607909888 | bytes 9754112 | tf_op jit(solution)/shard_map/lsd,de->lse/dot_general | solution.py:23
  100.7 11.0 %multiply_convert_fusion.1 = (bf16[8,256,1536]{2,1,0:T(8,128)(2,1)}, f32[8,256,1536]{2,1,0:T(8,128)}) fusion(f32[1536]{0:T(1024)} %reshape.150, bf16[384,1536]{1,0:T(8,128)(2,1)} %all-gather.7.cloned.1.call-done, f32[8,256,384]{2,1,0:T(8,128)} %copy-done.1, f32[8,384]{1,0:T(8,128)} %get-tuple-element.193, f32[8,384]{1,0:T(8,128)} %get-tuple-element.194, ...), kind=kOutput, calls=%fused_computation.69 | convolution fusion | flops 2451308544 | bytes 23246848 | tf_op jit(solution)/shard_map/lsd,de->lse/dot_general | solution.py:23
  111.7 15.0 %fusion.120 = (bf16[1536]{0:T(1024)(128)(2,1)}, bf16[8,256,1536]{2,1,0:T(8,128)(2,1)S(1)}) fusion(f32[8,256,1536]{2,1,0:T(8,128)} %get-tuple-element.206, f32[1536]{0:T(1024)} %reshape.150, bf16[1536,384]{1,0:T(8,128)(2,1)} %all-gather.9.cloned.1.call-done, bf16[8,256,384]{2,1,0:T(8,128)(2,1)} %param.29, f32[8,384]{1,0:T(8,128)} %get-tuple-element.192), kind=kOutput, calls=%fused_computation.169 | convolution fusion | flops 2487482880 | bytes 21648384 | tf_op jit(solution)/shard_map/lse,de->lsd/dot_general | solution.py:126
  126.9 3.6 fusion.92
  133.7 6.0 %fusion.79 = (bf16[8,384]{1,0:T(8,128)(2,1)}, bf16[8,256,384]{2,1,0:T(8,128)(2,1)}, bf16[8,384]{1,0:T(8,128)(2,1)}, f32[8,256]{1,0:T(8,128)S(1)}, f32[8,256]{1,0:T(8,128)S(1)}, /*index=5*/bf16[8,384]{1,0:T(8,128)(2,1)}) fusion(bf16[8,256,384]{2,1,0:T(8,128)(2,1)S(1)} %copy-done.13, f32[384]{0:T(512)S(1)} %copy-done.36, f32[8,256,384]{2,1,0:T(8,128)S(1)} %copy-done.2, ...), kind=kOutput, calls=%fused_computation.94 | convolution fusion | flops 2428488704 | bytes 16985600 | tf_op jit(solution)/shard_map/lsd,de->lse/dot_general | solution.py:23
  139.7 4.1 fusion.114
  146.6 3.7 convolution_convert_fusion.1
  150.4 2.6 copy.82
  157.0 37.3 %while.27 = (s32[]{:T(128)}, bf16[4,2,256,6,64]{2,4,3,1,0:T(8,128)(2,1)}, bf16[4,2,256,6,64]{2,4,3,1,0:T(8,128)(2,1)}, bf16[4,2,256,6,64]{2,4,3,1,0:T(8,128)(2,1...) while((s32[]{:T(128)}, ...), condition=%wide.region_12.13_spmd, body=%wide.region_10.12_spmd.sunk | while | flops 513733632 | bytes 33916044 | solution.py:141
  194.3 2.7 copy.85
  197.1 2.6 copy.83
  201.3 6.2 %fusion.82 = bf16[384,1152]{1,0:T(8,128)(2,1)} fusion(bf16[8,256,384]{2,1,0:T(8,128)(2,1)S(1)} %copy-done, f32[8,384]{1,0:T(8,128)S(1)} %copy-done.24, f32[8,384]{1,0:T(8,128)S(1)} %get-tuple-element.196, f32[8,256]{1,0:T(8,128)S(1)} %add_rsqrt_fusion.1, f32[8,256]{1,0:T(8,128)S(1)} %broadcast_multiply_fusion.5, bf16[8,256,384]{2,1,0:T(8,128)(2,1)} %copy.85, ...), kind=kOutput, calls=%fused_computation.111 | convolution fusion | flops 1831256064 | bytes 7217152 | tf_op jit(solution)/shard_map/lsd,lse->de/dot_general | solution.py:27
  207.6 7.6 %fusion.83 = bf16[384,1536]{1,0:T(8,128)(2,1)} fusion(bf16[8,256,1536]{2,1,0:T(8,128)(2,1)} %copy-done.39, f32[8,256,384]{2,1,0:T(8,128)} %copy-done.1, f32[8,384]{1,0:T(8,128)S(1)} %copy-done.29, f32[8,384]{1,0:T(8,128)S(1)} %copy-done.22, f32[8,256]{1,0:T(8,128)S(1)} %copy-done.26, f32[8,256]{1,0:T(8,128)S(1)} %broadcast_multiply_fusion.4), kind=kOutput, calls=%fused_computation.112 | convolution fusion | flops 2420441088 | bytes 10657792 | tf_op jit(solution)/shard_map/lsd,lse->de/dot_general | solution.py:27
  215.5 8.0 %fusion.84 = bf16[1536,384]{1,0:T(8,128)(2,1)} fusion(bf16[8,256,1536]{2,1,0:T(8,128)(2,1)} %get-tuple-element.205, bf16[8,256,384]{2,1,0:T(8,128)(2,1)} %param.29, f32[8,384]{1,0:T(8,128)S(1)} %copy-done.20), kind=kOutput, calls=%fused_computation.113 | convolution fusion | flops 2418868224 | bytes 9056256 | tf_op jit(solution)/shard_map/lsd,lse->de/dot_general | solution.py:27
  223.6 6.2 %fusion.76 = (bf16[8,384]{1,0:T(8,128)(2,1)S(1)}, f32[8,256]{1,0:T(8,128)S(1)}, f32[8,256]{1,0:T(8,128)S(1)}, bf16[8,384]{1,0:T(8,128)(2,1)S(1)}, f32[8,256,384]{2,1,0:T(8,128)S(1)}) fusion(bf16[8,256,384]{2,1,0:T(8,128)(2,1)S(1)} %copy-done, f32[8,256]{1,0:T(8,128)S(1)} %add_rsqrt_fusion.1, f32[8,256]{1,0:T(8,128)S(1)} %broadcast_multiply_fusion.5, ...), kind=kOutput, calls=%fused_computation.91 | convolution fusion | flops 1833949184 | bytes 10379264 | tf_op jit(solution)/shard_map/lse,de->lsd/dot_general | solution.py:155
  229.9 3.1 multiply_reduce_fusion.3
  235.2 24.6 %reduce-scatter.12.cloned.1.call-done = bf16[96,1536]{1,0:T(8,128)(2,1)} async-done(((bf16[384,1536]{1,0:T(8,128)(2,1)}), bf16[96,1536]{1,0:T(8,128)(2,1)}) %reduce-scatter.12.cloned.1.call-update) | async-done | bytes 294928 | tf_op jit(solution)/shard_map/reduce_scatter | solution.py:185
  259.8 28.5 %reduce-scatter.14.cloned.1.call-done = bf16[384,384]{1,0:T(8,128)(2,1)} async-done(((bf16[1536,384]{1,0:T(8,128)(2,1)}), bf16[384,384]{1,0:T(8,128)(2,1)}) %reduce-scatter.14.cloned.1.call-update) | async-done | bytes 294928 | tf_op jit(solution)/shard_map/reduce_scatter | solution.py:191
  288.3 32.0 %reduce-scatter.6.cloned.1.call-done = bf16[96,2304]{1,0:T(8,128)(2,1)} async-done(((bf16[384,2304]{1,0:T(8,128)(2,1)}), bf16[96,2304]{1,0:T(8,128)(2,1)}) %reduce-scatter.6.cloned.1.call-update) | async-done | bytes 442384 | tf_op jit(solution)/shard_map/reduce_scatter | solution.py:167
  325.2 10.5 %all-reduce.11 = (bf16[2304]{0:T(1024)(128)(2,1)S(1)}, bf16[768]{0:T(1024)(128)(2,1)S(1)}, bf16[384]{0:T(512)(128)(2,1)S(1)}, bf16[1536]{0:T(1024)(128)(2,1)S(1)}, bf16[384]{0:T(512)(128)(2,1)S(1)}) all-reduce(bf16[2304]{0:T(1024)(128)(2,1)S(1)} %reduce_sum.215, ...), channel_id=3, replica_groups=mesh['rep'=8,'shard'=4] {'shard'}, use_global_device_ids=true, to_apply=%region_24.25.clone | all-reduce | flops 5376 | bytes 21504
  336.1 22.2 %all-reduce.9 = (bf16[576]{0:T(1024)(128)(2,1)S(1)}, bf16[192]{0:T(256)(128)(2,1)S(1)}, bf16[96]{0:T(256)(128)(2,1)S(1)}, bf16[384]{0:T(512)(128)(2,1)S(1)}, bf16[96]{0:T(256)(128)(2,1)S(1)}) all-reduce(bf16[576]{0:T(1024)(128)(2,1)S(1)} %dynamic-slice.5, ...), channel_id=1, replica_groups=mesh['rep'=8,'shard'=4] {'rep'}, use_global_device_ids=true, to_apply=%region_25.26 | all-reduce | flops 1344 | bytes 5376 | tf_op jit(solution)/shard_map/psum | solution.py:200
  362.3 47.9 %all-reduce.15.cloned.1.call-done = (bf16[96,2304]{1,0:T(8,128)(2,1)}, bf16[96,1152]{1,0:T(8,128)(2,1)}, bf16[96,384]{1,0:T(8,128)(2,1)}, bf16[96,1536]{1,0:T(8,128)(2,1)}, bf16[384,384]{1,0:T(8,128)(2,1)}) async-done(((bf16[96,2304]{1,0:T(8,128)(2,1)}, bf16[96,1152]{1,0:T(8,128)(2,1)}, bf16[96,384]{1,0:T(8,128)(2,1)}, bf16[96,1536]{1,0:T(8,128)(2,1)}, bf16[384,384]{1,0:T(8,128)(2,1)}), ...) | async-done | bytes 1327120 | tf_op jit(solution)/shard_map/psum | solution.py:199
  (218 shorter events, 103.9 us)
Async XLA Ops:
  7.2 31.1 %copy-start = (bf16[8,256,384]{2,1,0:T(8,128)(2,1)S(1)}, bf16[8,256,384]{2,1,0:T(8,128)(2,1)}, u32[]{:S(2)}) copy-start(bf16[8,256,384]{2,1,0:T(8,128)(2,1)} %param.17) | copy-start | bytes 4718596
  7.2 32.0 %copy-start.16 = (bf16[96,384]{1,0:T(8,128)(2,1)S(1)}, bf16[96,384]{1,0:T(8,128)(2,1)}, u32[]{:S(2)}) copy-start(bf16[96,384]{1,0:T(8,128)(2,1)} %param.23) | copy-start | bytes 221188
  7.2 37.9 %copy-start.15 = (bf16[96,1152]{1,0:T(8,128)(2,1)S(1)}, bf16[96,1152]{1,0:T(8,128)(2,1)}, u32[]{:S(2)}) copy-start(bf16[96,1152]{1,0:T(8,128)(2,1)} %param.21) | copy-start | bytes 663556
  7.2 49.2 %copy-start.17 = (bf16[8,384]{1,0:T(8,128)(2,1)S(1)}, bf16[8,384]{1,0:T(8,128)(2,1)}, u32[]{:S(2)}) copy-start(bf16[8,384]{1,0:T(8,128)(2,1)} %param.18) | copy-start | bytes 18436
  7.2 49.2 %all-gather.5.cloned.1.call-start = ((), (), s32[]{:S(2)}) async-start(), calls=%async_computation.5 | async-start | bytes 2211840 | tf_op jit(solution)/shard_map/all_gather | solution.py:74
  8.0 92.7 %all-gather.7.cloned.1.call-start = ((), (), s32[]{:S(2)}) async-start(), calls=%async_computation.6 | async-start | bytes 1474560 | tf_op jit(solution)/shard_map/all_gather | solution.py:80
  8.7 103.0 %all-gather.9.cloned.1.call-start = ((), (), s32[]{:S(2)}) async-start(), calls=%async_computation.7 | async-start | bytes 1474560 | tf_op jit(solution)/shard_map/all_gather | solution.py:82
  9.4 225.7 %reduce-scatter.10.cloned.1.call-start = ((), (), s32[]{:S(2)}) async-start(), calls=%async_computation.10 | async-start | bytes 368640 | tf_op jit(solution)/shard_map/reduce_scatter | solution.py:179
  35.9 57.2 %copy-start.27 = (f32[384]{0:T(512)}, f32[384]{0:T(512)S(1)}, u32[]{:S(2)}) copy-start(f32[384]{0:T(512)S(1)} %convert_element_type.177) | copy-start | bytes 4612
  56.4 5.8 %copy-start.12 = (bf16[384,1152]{1,0:T(8,128)(2,1)}, bf16[384,1152]{1,0:T(8,128)(2,1)S(1)}, u32[]{:S(2)}) copy-start(bf16[384,1152]{1,0:T(8,128)(2,1)S(1)} %all_gather.37) | copy-start | bytes 2654212
  111.7 15.1 %copy-start.38 = (bf16[384,1536]{1,0:T(8,128)(2,1)S(1)}, bf16[384,1536]{1,0:T(8,128)(2,1)}, u32[]{:S(2)}) copy-start(bf16[384,1536]{1,0:T(8,128)(2,1)} %all-gather.7.cloned.1.call-done) | copy-start | bytes 3538948
  126.8 6.8 %copy-start.40 = (bf16[8,256,1536]{2,1,0:T(8,128)(2,1)S(1)}, bf16[8,256,1536]{2,1,0:T(8,128)(2,1)}, u32[]{:S(2)}) copy-start(bf16[8,256,1536]{2,1,0:T(8,128)(2,1)} %get-tuple-element.205) | copy-start | bytes 18874372
  150.3 84.8 %reduce-scatter.8.cloned.1.call-start = ((), (), s32[]{:S(2)}) async-start(), calls=%async_computation.9 | async-start | bytes 1105920 | tf_op jit(solution)/shard_map/reduce_scatter | solution.py:173
  194.3 5.3 %copy-start.8 = (bf16[4,2,256,6,64]{2,4,3,1,0:T(8,128)(2,1)S(1)}, bf16[4,2,256,6,64]{2,4,3,1,0:T(8,128)(2,1)}, u32[]{:S(2)}) copy-start(bf16[4,2,256,6,64]{2,4,3,1,0:T(8,128)(2,1)} %get-tuple-element.98) | copy-start | bytes 4718596
  201.3 6.3 %copy-start.22 = (f32[8,384]{1,0:T(8,128)S(1)}, f32[8,384]{1,0:T(8,128)}, u32[]{:S(2)}) copy-start(f32[8,384]{1,0:T(8,128)} %get-tuple-element.194) | copy-start | bytes 36868
  201.3 6.3 %copy-start.26 = (f32[8,256]{1,0:T(8,128)S(1)}, f32[8,256]{1,0:T(8,128)}, u32[]{:S(2)}) copy-start(f32[8,256]{1,0:T(8,128)} %add_rsqrt_fusion) | copy-start | bytes 24580
  201.3 6.3 %copy-start.29 = (f32[8,384]{1,0:T(8,128)S(1)}, f32[8,384]{1,0:T(8,128)}, u32[]{:S(2)}) copy-start(f32[8,384]{1,0:T(8,128)} %get-tuple-element.193) | copy-start | bytes 36868
  207.5 8.0 %copy-start.20 = (f32[8,384]{1,0:T(8,128)S(1)}, f32[8,384]{1,0:T(8,128)}, u32[]{:S(2)}) copy-start(f32[8,384]{1,0:T(8,128)} %get-tuple-element.192) | copy-start | bytes 36868
  207.5 52.3 %reduce-scatter.12.cloned.1.call-start = ((), (), s32[]{:S(2)}) async-start(), calls=%async_computation.11 | async-start | bytes 1474560 | tf_op jit(solution)/shard_map/reduce_scatter | solution.py:185
  215.2 8.3 %copy-start.10 = (bf16[8,256,384]{2,1,0:T(8,128)(2,1)S(1)}, bf16[8,256,384]{2,1,0:T(8,128)(2,1)}, u32[]{:S(2)}) copy-start(bf16[8,256,384]{2,1,0:T(8,128)(2,1)} %copy.85) | copy-start | bytes 4718596
  215.2 73.0 %reduce-scatter.14.cloned.1.call-start = ((), (), s32[]{:S(2)}) async-start(), calls=%async_computation.12 | async-start | bytes 1474560 | tf_op jit(solution)/shard_map/reduce_scatter | solution.py:191
  223.5 6.3 %copy-start.28 = (f32[384]{0:T(512)S(1)}, f32[384]{0:T(512)}, u32[]{:S(2)}) copy-start(f32[384]{0:T(512)} %copy-done.27) | copy-start | bytes 4612
  223.5 96.8 %reduce-scatter.6.cloned.1.call-start = ((), (), s32[]{:S(2)}) async-start(), calls=%async_computation.8 | async-start | bytes 2211840 | tf_op jit(solution)/shard_map/reduce_scatter | solution.py:167
  223.6 6.2 %copy-start.4 = (f32[8,256,384]{2,1,0:T(8,128)S(1)}, f32[8,256,384]{2,1,0:T(8,128)}, u32[]{:S(2)}) copy-start(f32[8,256,384]{2,1,0:T(8,128)} %get-tuple-element.204) | copy-start | bytes 9437188
  223.6 6.2 %copy-start.5 = (f32[8,256,384]{2,1,0:T(8,128)S(1)}, f32[8,256,384]{2,1,0:T(8,128)}, u32[]{:S(2)}) copy-start(f32[8,256,384]{2,1,0:T(8,128)} %get-tuple-element.174) | copy-start | bytes 9437188
  233.0 89.9 %copy-start.11 = (bf16[8,256,384]{2,1,0:T(8,128)(2,1)S(1)}, bf16[8,256,384]{2,1,0:T(8,128)(2,1)}, u32[]{:S(2)}) copy-start(bf16[8,256,384]{2,1,0:T(8,128)(2,1)} %copy.85) | copy-start | bytes 4718596
  235.0 90.2 %copy-start.33 = (bf16[384]{0:T(512)(128)(2,1)S(1)}, bf16[384]{0:T(512)(128)(2,1)}, u32[]{:S(2)}) copy-start(bf16[384]{0:T(512)(128)(2,1)} %get-tuple-element.172) | copy-start | bytes 2308
  235.0 90.2 %copy-start.34 = (bf16[384]{0:T(512)(128)(2,1)S(1)}, bf16[384]{0:T(512)(128)(2,1)}, u32[]{:S(2)}) copy-start(bf16[384]{0:T(512)(128)(2,1)} %get-tuple-element.191) | copy-start | bytes 2308
  235.0 90.2 %copy-start.35 = (bf16[1536]{0:T(1024)(128)(2,1)S(1)}, bf16[1536]{0:T(1024)(128)(2,1)}, u32[]{:S(2)}) copy-start(bf16[1536]{0:T(1024)(128)(2,1)} %get-tuple-element.208) | copy-start | bytes 9220
  235.0 126.1 %copy-start.6 = (bf16[384,2304]{1,0:T(8,128)(2,1)S(1)}, bf16[384,2304]{1,0:T(8,128)(2,1)}, u32[]{:S(2)}) copy-start(bf16[384,2304]{1,0:T(8,128)(2,1)} %all-gather.5.cloned.1.call-done) | copy-start | bytes 5308420
  235.1 175.2 %all-reduce.15.cloned.1.call-start = ((), (), s32[]{:S(2)}) async-start(), calls=%async_computation.13 | async-start | bytes 2654208 | tf_op jit(solution)/shard_map/psum | solution.py:199
  410.2 7.1 %copy-start.14 = (bf16[384,384]{1,0:T(8,128)(2,1)S(1)}, bf16[384,384]{1,0:T(8,128)(2,1)}, u32[]{:S(2)}) copy-start(bf16[384,384]{1,0:T(8,128)(2,1)} %get-tuple-element.162) | copy-start | bytes 884740
  (21 other events, 71.0 us)
Sparse Core Ops, SparseCore 0:
  9.6 23.5 all-gather.4
  34.8 19.2 all-gather.6
  55.6 17.1 all-gather.8
  150.4 20.4 reduce-scatter.9
  207.6 23.9 reduce-scatter.7
  234.0 25.7 reduce-scatter.11
  262.5 25.7 reduce-scatter.13
  290.9 29.3 reduce-scatter.5
  324.8 85.3 all-reduce.14
where the time goes:
time: 429 us; the launch traced here: 425 us
  waiting for transfers between devices  135 us (31%)
  matrix products  133 us (31%)
  blocking collectives  68.3 us (16%)
  local copies, waits for them, and re-layouts  35.9 us (8%)
  other arithmetic  33 us (8%)
  between operations  19.2 us (4%)
    psum x1, waiting for transfers between devices, on_device(): lax.psum(partial_value[0].astype(jnp.bfloat16), 'rep').astype(jnp.float32)  47.9 us
    reduce_scatter x1, waiting for transfers between devices, on_device(): lax.psum_scatter(gw_ada.astype(jnp.bfloat16), 'shard', scatter_dimension=...  32 us
    reduce_scatter x1, waiting for transfers between devices, on_device(): lax.psum_scatter(gw_2.astype(jnp.bfloat16), 'shard', scatter_dimension=0,...  28.5 us
    dot_general x4, matrix products, project(): jnp.einsum('lsd,de->lse', left, right, preferred_element_type=jnp.float32)  24.6 us
    reduce_scatter x1, waiting for transfers between devices, on_device(): lax.psum_scatter(gw_1.astype(jnp.bfloat16), 'shard', scatter_dimension=0,...  24.6 us
    dot_general x4, matrix products, weight_grad(): jnp.einsum('lsd,lse->de', left, right, preferred_element_type=jnp.float32)  23.4 us
    unnamed x2, blocking collectives  22.9 us
    psum x1, blocking collectives, on_device(): lax.psum(partial_value[1].astype(jnp.bfloat16), 'rep').astype(jnp.float32)  22.2 us
  transfers between devices with their start and end apart: 9, of which 4 were waited for; matrix products, arithmetic and copies ran while one was open for 36% of the time, Pallas kernels for 0%

commit v1 on v0

--- a/solution.py
+++ b/solution.py
@@ -5,6 +5,22 @@
 from jax.sharding import PartitionSpec as P
 
 HEADS = 6
+
+
+def link_the_shards(x_local):
+    lanes = lax.axis_size("shard")
+    line_up = list(map(lambda dev_i: (dev_i, (dev_i + 1) % lanes), range(lanes)))
+    shelf = list(map(lambda dev_i: (dev_i, (dev_i - 1) % lanes), range(lanes)))
+    local_part, z1 = ([x_local], [x_local])
+    for _ in range(lanes // 2):
+        local_part.append(lax.ppermute(local_part[-1], "shard", line_up))
+    for _ in range((lanes - 1) // 2):
+        z1.append(lax.ppermute(z1[-1], "shard", shelf))
+    return jnp.roll(
+        jnp.concatenate([*local_part[::-1], *z1[1:]], axis=0),
+        (lax.axis_index("shard") - lanes // 2) * x_local.shape[0],
+        axis=0,
+    )
 
 
 def layer_norm(value):
@@ -73,7 +89,7 @@
     whole = (
         lax.all_gather(w_ada, "shard", axis=0, tiled=True),
         lax.all_gather(b_ada, "shard", axis=0, tiled=True),
-        lax.all_gather(w_qkv, "shard", axis=0, tiled=True),
+        link_the_shards(w_qkv),
         lax.all_gather(b_qv, "shard", axis=0, tiled=True),
         lax.all_gather(w_o, "shard", axis=0, tiled=True),
         lax.all_gather(b_o, "shard", axis=0, tiled=True),

time: 429 us -> 451 us (1.051)
  waiting for transfers between devices: 135 us -> 151 us
    ppermute x0 -> x3, waiting for transfers between devices: none -> 6.86 us  [the longest x2 6.86 us: link_the_shards(): local_part.append(lax.ppermute(local_part[-1], 'shard', line_up))]
    reduce_scatter x1, waiting for transfers between devices: 0.02 us -> 5.56 us  [on_device(): lax.psum_scatter(gw_qkv.astype(jnp.bfloat16), 'shard', scatter_dimension=...]
    unnamed x100 -> x107, local copies, waits for them, and re-layouts: 12 us -> 15.1 us
  transfers between devices with their start and end apart: 9 -> 12, of which waited for: 4 -> 6; matrix products, arithmetic and copies ran while one was open for 36% -> 24% of each run, Pallas kernels for 0% -> 0%
where the time goes in v1:
time: 451 us; the launch traced here: 444 us
  waiting for transfers between devices  151 us (33%)
  matrix products  132 us (29%)
  blocking collectives  66.4 us (15%)
  local copies, waits for them, and re-layouts  39.9 us (9%)
  other arithmetic  32.3 us (7%)
  between operations  19.4 us (4%)
    psum x1, waiting for transfers between devices, on_device(): lax.psum(partial_value[0].astype(jnp.bfloat16), 'rep').astype(jnp.float32)  48 us
    reduce_scatter x1, waiting for transfers between devices, on_device(): lax.psum_scatter(gw_ada.astype(jnp.bfloat16), 'shard', scatter_dimension=...  32 us
    reduce_scatter x1, waiting for transfers between devices, on_device(): lax.psum_scatter(gw_2.astype(jnp.bfloat16), 'shard', scatter_dimension=0,...  28.5 us
    reduce_scatter x1, waiting for transfers between devices, on_device(): lax.psum_scatter(gw_1.astype(jnp.bfloat16), 'shard', scatter_dimension=0,...  28.2 us
    dot_general x4, matrix products, project(): jnp.einsum('lsd,de->lse', left, right, preferred_element_type=jnp.float32)  25.9 us
    dot_general x4, matrix products, weight_grad(): jnp.einsum('lsd,lse->de', left, right, preferred_element_type=jnp.float32)  23.8 us
    psum x1, blocking collectives, on_device(): lax.psum(partial_value[1].astype(jnp.bfloat16), 'rep').astype(jnp.float32)  22.2 us
    unnamed x2, blocking collectives  22.1 us
  transfers between devices with their start and end apart: 12, of which 6 were waited for; matrix products, arithmetic and copies ran while one was open for 24% of the time, Pallas kernels for 0%

profile of v1, /device:TPU:0, one launch (start us, length us, event | category | flops | bytes accessed | tf_op | source)
XLA Modules:
  0.0 444.3 jit_solution(2811673916843557214)
XLA Ops:
  18.1 11.6 %all-reduce.12 = (bf16[2304]{0:T(1024)(128)(2,1)S(1)}, bf16[768]{0:T(1024)(128)(2,1)S(1)}, bf16[384]{0:T(512)(128)(2,1)S(1)}, bf16[384]{0:T(512)(128)(2,1)S(1)}) all-reduce(bf16[2304]{0:T(1024)(128)(2,1)S(1)} %dynamic-update-slice, bf16[768]{0:T(1024)(128)(2,1)S(1)} %dynamic-update-slice.1, ...), channel_id=1, replica_groups=mesh['rep'=8,'shard'=4] {'shard'}, use_global_device_ids=true, to_apply=%add | all-reduce | flops 3840 | bytes 15360
  33.0 6.2 %all_gather.37 = bf16[384,384]{1,0:T(8,128)(2,1)S(1)} all-gather(bf16[96,384]{1,0:T(8,128)(2,1)S(1)} %copy-done.13), channel_id=1, replica_groups=mesh['rep'=8,'shard'=4] {'shard'}, dimensions={0}, use_global_device_ids=true | all-gather | bytes 368640 | tf_op jit(solution)/shard_map/all_gather | solution.py:94
  39.2 5.1 %all-gather = bf16[4,1,384]{2,1,0:T(2,128)(2,1)S(1)} all-gather(bf16[1,1,384]{2,1,0:T(2,128)(2,1)S(1)} %reshape.148), channel_id=1, replica_groups=mesh['rep'=8,'shard'=4] {'shard'}, dimensions={0}, use_global_device_ids=true | all-gather | bytes 3840 | tf_op jit(solution)/shard_map/all_gather | solution.py:97
  46.5 6.9 %collective-permute-done.1 = bf16[96,1152]{1,0:T(8,128)(2,1)S(1)} collective-permute-done((bf16[96,1152]{1,0:T(8,128)(2,1)S(1)}, bf16[96,1152]{1,0:T(8,128)(2,1)S(1)}, u32[]{:S(2)}, u32[]{:S(2)}) %collective-permute-start.1) | collective-permute-done | bytes 221216 | tf_op jit(solution)/shard_map/ppermute | solution.py:16
  61.4 4.2 fusion.98
  72.7 2.6 copy.80
  76.7 18.9 %while.26 = (s32[]{:T(128)}, bf16[4,2,256,6,64]{2,4,3,1,0:T(8,128)(2,1)}, f32[4,2,6,256,1]{3,2,1,4,0:T(8,128)S(1)}, bf16[4,2,256,6,64]{2,4,3,1,0:T(8,128)(2,1)},...) while((s32[]{:T(128)}, ...), condition=%wide.region_5.6_spmd, body=%wide.region_2.5_spmd.sunk | while | flops 208598016 | bytes 11122769 | solution.py:118
  83.6 2.5 fusion.154
  95.6 4.6 %fusion.117 = (f32[8,256]{1,0:T(8,128)S(1)}, f32[8,256,384]{2,1,0:T(8,128)S(1)}, f32[8,256,384]{2,1,0:T(8,128)}) fusion(f32[384]{0:T(512)S(1)} %copy-done.24, f32[8,384]{1,0:T(8,128)S(1)} %get-tuple-element.197, bf16[8,256,384]{2,1,0:T(8,128)(2,1)S(1)} %copy-done, bf16[8,256,384]{1,2,0:T(8,128)(2,1)} %bitcast.23, bf16[384,384]{1,0:T(8,128)(2,1)S(1)} %all_gather.37), kind=kOutput, calls=%fused_computation.174 | convolution fusion | flops 607909888 | bytes 9754112 | tf_op jit(solution)/shard_map/lsd,de->lse/dot_general | solution.py:39
  103.1 11.0 %multiply_convert_fusion.1 = (bf16[8,256,1536]{2,1,0:T(8,128)(2,1)}, f32[8,256,1536]{2,1,0:T(8,128)}) fusion(f32[1536]{0:T(1024)} %reshape.150, bf16[384,1536]{1,0:T(8,128)(2,1)} %all-gather.7.cloned.1.call-done, f32[8,256,384]{2,1,0:T(8,128)} %copy-done.1, f32[8,384]{1,0:T(8,128)} %get-tuple-element.193, f32[8,384]{1,0:T(8,128)} %get-tuple-element.194, ...), kind=kOutput, calls=%fused_computation.69 | convolution fusion | flops 2451308544 | bytes 23246848 | tf_op jit(solution)/shard_map/lsd,de->lse/dot_general | solution.py:39
  114.2 14.8 %fusion.122 = (bf16[1536]{0:T(1024)(128)(2,1)}, bf16[8,256,1536]{2,1,0:T(8,128)(2,1)S(1)}) fusion(f32[8,256,1536]{2,1,0:T(8,128)} %get-tuple-element.206, f32[1536]{0:T(1024)} %reshape.150, bf16[1536,384]{1,0:T(8,128)(2,1)} %all-gather.9.cloned.1.call-done, bf16[8,256,384]{2,1,0:T(8,128)(2,1)} %param.29, f32[8,384]{1,0:T(8,128)} %get-tuple-element.192), kind=kOutput, calls=%fused_computation.179 | convolution fusion | flops 2487482880 | bytes 21648384 | tf_op jit(solution)/shard_map/lse,de->lsd/dot_general | solution.py:142
  129.0 3.6 fusion.92
  135.9 6.0 %fusion.79 = (bf16[8,384]{1,0:T(8,128)(2,1)}, bf16[8,256,384]{2,1,0:T(8,128)(2,1)}, bf16[8,384]{1,0:T(8,128)(2,1)}, f32[8,256]{1,0:T(8,128)S(1)}, f32[8,256]{1,0:T(8,128)S(1)}, /*index=5*/bf16[8,384]{1,0:T(8,128)(2,1)}) fusion(bf16[8,256,384]{2,1,0:T(8,128)(2,1)S(1)} %copy-done.10, f32[384]{0:T(512)S(1)} %copy-done.35, f32[8,256,384]{2,1,0:T(8,128)S(1)} %copy-done.2, ...), kind=kOutput, calls=%fused_computation.94 | convolution fusion | flops 2428488704 | bytes 16985600 | tf_op jit(solution)/shard_map/lsd,de->lse/dot_general | solution.py:39
  141.9 4.1 fusion.116
  148.3 3.1 fusion.85
  151.4 2.6 copy.82
  158.0 37.4 %while.27 = (s32[]{:T(128)}, bf16[4,2,256,6,64]{2,4,3,1,0:T(8,128)(2,1)}, bf16[4,2,256,6,64]{2,4,3,1,0:T(8,128)(2,1)}, bf16[4,2,256,6,64]{2,4,3,1,0:T(8,128)(2,1...) while((s32[]{:T(128)}, ...), condition=%wide.region_12.13_spmd, body=%wide.region_10.12_spmd.sunk | while | flops 513733632 | bytes 33916036 | solution.py:157
  195.4 2.8 copy.83
  199.7 2.7 copy.85
  202.6 5.3 %fusion.82 = bf16[384,1152]{1,0:T(8,128)(2,1)} fusion(bf16[8,256,384]{2,1,0:T(8,128)(2,1)S(1)} %copy-done, f32[8,384]{1,0:T(8,128)S(1)} %copy-done.21, f32[8,384]{1,0:T(8,128)S(1)} %get-tuple-element.196, f32[8,256]{1,0:T(8,128)S(1)} %add_rsqrt_fusion.1, f32[8,256]{1,0:T(8,128)S(1)} %broadcast_multiply_fusion.5, bf16[8,256,384]{2,1,0:T(8,128)(2,1)} %copy.85, ...), kind=kOutput, calls=%fused_computation.111 | convolution fusion | flops 1831256064 | bytes 7217152 | tf_op jit(solution)/shard_map/lsd,lse->de/dot_general | solution.py:43
  208.0 7.7 %fusion.83 = bf16[384,1536]{1,0:T(8,128)(2,1)} fusion(bf16[8,256,1536]{2,1,0:T(8,128)(2,1)} %copy-done.39, f32[8,256,384]{2,1,0:T(8,128)} %copy-done.1, f32[8,384]{1,0:T(8,128)S(1)} %copy-done.26, f32[8,384]{1,0:T(8,128)S(1)} %copy-done.19, f32[8,256]{1,0:T(8,128)S(1)} %copy-done.23, f32[8,256]{1,0:T(8,128)S(1)} %broadcast_multiply_fusion.4), kind=kOutput, calls=%fused_computation.112 | convolution fusion | flops 2420441088 | bytes 10657792 | tf_op jit(solution)/shard_map/lsd,lse->de/dot_general | solution.py:43
  215.7 10.8 %all_gather.43 = bf16[384,1152]{1,0:T(8,128)(2,1)} all-gather(bf16[96,1152]{1,0:T(8,128)(2,1)} %param.21), channel_id=1, replica_groups=mesh['rep'=8,'shard'=4] {'shard'}, dimensions={0}, use_global_device_ids=true | all-gather | bytes 1105920 | tf_op jit(solution)/shard_map/all_gather | solution.py:131
  226.6 7.7 %fusion.84 = bf16[1536,384]{1,0:T(8,128)(2,1)} fusion(bf16[8,256,1536]{2,1,0:T(8,128)(2,1)} %get-tuple-element.205, bf16[8,256,384]{2,1,0:T(8,128)(2,1)} %param.29, f32[8,384]{1,0:T(8,128)S(1)} %copy-done.17), kind=kOutput, calls=%fused_computation.113 | convolution fusion | flops 2418868224 | bytes 9056256 | tf_op jit(solution)/shard_map/lsd,lse->de/dot_general | solution.py:43
  234.4 6.2 %fusion.76 = (bf16[8,384]{1,0:T(8,128)(2,1)S(1)}, f32[8,256]{1,0:T(8,128)S(1)}, f32[8,256]{1,0:T(8,128)S(1)}, bf16[8,384]{1,0:T(8,128)(2,1)S(1)}, f32[8,256,384]{2,1,0:T(8,128)S(1)}) fusion(bf16[8,256,384]{2,1,0:T(8,128)(2,1)S(1)} %copy-done, f32[8,256]{1,0:T(8,128)S(1)} %add_rsqrt_fusion.1, f32[8,256]{1,0:T(8,128)S(1)} %broadcast_multiply_fusion.5, ...), kind=kOutput, calls=%fused_computation.91 | convolution fusion | flops 1833949184 | bytes 10379264 | tf_op jit(solution)/shard_map/lse,de->lsd/dot_general | solution.py:171
  240.7 3.1 multiply_reduce_fusion.3
  246.0 5.6 %reduce-scatter.8.cloned.1.call-done = bf16[96,1152]{1,0:T(8,128)(2,1)} async-done(((bf16[384,1152]{1,0:T(8,128)(2,1)}), bf16[96,1152]{1,0:T(8,128)(2,1)}) %reduce-scatter.8.cloned.1.call-update) | async-done | bytes 221200 | tf_op jit(solution)/shard_map/reduce_scatter | solution.py:189
  251.5 28.2 %reduce-scatter.12.cloned.1.call-done = bf16[96,1536]{1,0:T(8,128)(2,1)} async-done(((bf16[384,1536]{1,0:T(8,128)(2,1)}), bf16[96,1536]{1,0:T(8,128)(2,1)}) %reduce-scatter.12.cloned.1.call-update) | async-done | bytes 294928 | tf_op jit(solution)/shard_map/reduce_scatter | solution.py:201
  279.7 28.5 %reduce-scatter.14.cloned.1.call-done = bf16[384,384]{1,0:T(8,128)(2,1)} async-done(((bf16[1536,384]{1,0:T(8,128)(2,1)}), bf16[384,384]{1,0:T(8,128)(2,1)}) %reduce-scatter.14.cloned.1.call-update) | async-done | bytes 294928 | tf_op jit(solution)/shard_map/reduce_scatter | solution.py:207
  308.2 32.0 %reduce-scatter.6.cloned.1.call-done = bf16[96,2304]{1,0:T(8,128)(2,1)} async-done(((bf16[384,2304]{1,0:T(8,128)(2,1)}), bf16[96,2304]{1,0:T(8,128)(2,1)}) %reduce-scatter.6.cloned.1.call-update) | async-done | bytes 442384 | tf_op jit(solution)/shard_map/reduce_scatter | solution.py:183
  345.2 10.5 %all-reduce.11 = (bf16[2304]{0:T(1024)(128)(2,1)S(1)}, bf16[768]{0:T(1024)(128)(2,1)S(1)}, bf16[384]{0:T(512)(128)(2,1)S(1)}, bf16[1536]{0:T(1024)(128)(2,1)S(1)}, bf16[384]{0:T(512)(128)(2,1)S(1)}) all-reduce(bf16[2304]{0:T(1024)(128)(2,1)S(1)} %reduce_sum.215, ...), channel_id=3, replica_groups=mesh['rep'=8,'shard'=4] {'shard'}, use_global_device_ids=true, to_apply=%region_24.25.clone | all-reduce | flops 5376 | bytes 21504
  356.1 22.2 %all-reduce.9 = (bf16[576]{0:T(1024)(128)(2,1)S(1)}, bf16[192]{0:T(256)(128)(2,1)S(1)}, bf16[96]{0:T(256)(128)(2,1)S(1)}, bf16[384]{0:T(512)(128)(2,1)S(1)}, bf16[96]{0:T(256)(128)(2,1)S(1)}) all-reduce(bf16[576]{0:T(1024)(128)(2,1)S(1)} %dynamic-slice.5, ...), channel_id=1, replica_groups=mesh['rep'=8,'shard'=4] {'rep'}, use_global_device_ids=true, to_apply=%region_25.26 | all-reduce | flops 1344 | bytes 5376 | tf_op jit(solution)/shard_map/psum | solution.py:216
  382.2 48.0 %all-reduce.15.cloned.1.call-done = (bf16[96,2304]{1,0:T(8,128)(2,1)}, bf16[96,1152]{1,0:T(8,128)(2,1)}, bf16[96,384]{1,0:T(8,128)(2,1)}, bf16[96,1536]{1,0:T(8,128)(2,1)}, bf16[384,384]{1,0:T(8,128)(2,1)}) async-done(((bf16[96,2304]{1,0:T(8,128)(2,1)}, bf16[96,1152]{1,0:T(8,128)(2,1)}, bf16[96,384]{1,0:T(8,128)(2,1)}, bf16[96,1536]{1,0:T(8,128)(2,1)}, bf16[384,384]{1,0:T(8,128)(2,1)}), ...) | async-done | bytes 1327120 | tf_op jit(solution)/shard_map/psum | solution.py:215
  (232 shorter events, 114.4 us)
Async XLA Ops:
  7.2 47.5 %copy-start.9 = (bf16[96,1152]{1,0:T(8,128)(2,1)S(1)}, bf16[96,1152]{1,0:T(8,128)(2,1)}, u32[]{:S(2)}) copy-start(bf16[96,1152]{1,0:T(8,128)(2,1)} %param.21) | copy-start | bytes 663556
  7.2 24.3 %copy-start = (bf16[8,256,384]{2,1,0:T(8,128)(2,1)S(1)}, bf16[8,256,384]{2,1,0:T(8,128)(2,1)}, u32[]{:S(2)}) copy-start(bf16[8,256,384]{2,1,0:T(8,128)(2,1)} %param.17) | copy-start | bytes 4718596
  7.2 25.8 %copy-start.13 = (bf16[96,384]{1,0:T(8,128)(2,1)S(1)}, bf16[96,384]{1,0:T(8,128)(2,1)}, u32[]{:S(2)}) copy-start(bf16[96,384]{1,0:T(8,128)(2,1)} %param.23) | copy-start | bytes 221188
  7.2 31.9 %copy-start.36 = (bf16[384]{0:T(512)(128)(2,1)S(1)}, bf16[384]{0:T(512)(128)(2,1)}, u32[]{:S(2)}) copy-start(bf16[384]{0:T(512)(128)(2,1)} %param.26) | copy-start | bytes 2308
  7.2 51.7 %all-gather.5.cloned.1.call-start = ((), (), s32[]{:S(2)}) async-start(), calls=%async_computation.5 | async-start | bytes 2211840 | tf_op jit(solution)/shard_map/all_gather | solution.py:90
  8.0 95.2 %all-gather.7.cloned.1.call-start = ((), (), s32[]{:S(2)}) async-start(), calls=%async_computation.6 | async-start | bytes 1474560 | tf_op jit(solution)/shard_map/all_gather | solution.py:96
  8.7 105.5 %all-gather.9.cloned.1.call-start = ((), (), s32[]{:S(2)}) async-start(), calls=%async_computation.7 | async-start | bytes 1474560 | tf_op jit(solution)/shard_map/all_gather | solution.py:98
  8.8 36.8 %collective-permute-start = (bf16[96,1152]{1,0:T(8,128)(2,1)}, bf16[96,1152]{1,0:T(8,128)(2,1)S(1)}, u32[]{:S(2)}, u32[]{:S(2)}) collective-permute-start(bf16[96,1152]{1,0:T(8,128)(2,1)} %param.21), channel_id=1, source_target_pairs={{0,1},{1,2},{2,3},{3,0},{4,5},{5,6},{6,7},{7,4},{8,9},{9,10},{10,1... | collective-permute-start | bytes 663560 | tf_op jit(solution)/shard_map/ppermute | solution.py:16
  9.3 46.2 %collective-permute-start.2 = (bf16[96,1152]{1,0:T(8,128)(2,1)}, bf16[96,1152]{1,0:T(8,128)(2,1)S(1)}, u32[]{:S(2)}, u32[]{:S(2)}) collective-permute-start(bf16[96,1152]{1,0:T(8,128)(2,1)} %param.21), channel_id=1, source_target_pairs={{0,3},{1,0},{2,1},{3,2},{4,7},{5,4},{6,5},{7,6},{8,11},{9,8},{10,9... | collective-permute-start | bytes 663560 | tf_op jit(solution)/shard_map/ppermute | solution.py:18
  11.3 234.7 %reduce-scatter.10.cloned.1.call-start = ((), (), s32[]{:S(2)}) async-start(), calls=%async_computation.10 | async-start | bytes 368640 | tf_op jit(solution)/shard_map/reduce_scatter | solution.py:195
  31.5 27.5 %copy-start.14 = (bf16[8,384]{1,0:T(8,128)(2,1)S(1)}, bf16[8,384]{1,0:T(8,128)(2,1)}, u32[]{:S(2)}) copy-start(bf16[8,384]{1,0:T(8,128)(2,1)} %param.18) | copy-start | bytes 18436
  45.5 7.8 %collective-permute-start.1 = (bf16[96,1152]{1,0:T(8,128)(2,1)S(1)}, bf16[96,1152]{1,0:T(8,128)(2,1)S(1)}, u32[]{:S(2)}, u32[]{:S(2)}) collective-permute-start(bf16[96,1152]{1,0:T(8,128)(2,1)S(1)} %collective-permute-done), channel_id=1, source_target_pairs={{0,1},{1,2},{2,3},{3,0},{4,5},{5,6},{6,7},{7,4},{8,9},{9,10},{10,1... | collective-permute-start | bytes 663560 | tf_op jit(solution)/shard_map/ppermute | solution.py:16
  76.6 18.9 %copy-start.24 = (f32[384]{0:T(512)S(1)}, f32[384]{0:T(512)}, u32[]{:S(2)}) copy-start(f32[384]{0:T(512)} %convert_element_type.177) | copy-start | bytes 4612
  114.2 14.8 %copy-start.37 = (bf16[384,1536]{1,0:T(8,128)(2,1)S(1)}, bf16[384,1536]{1,0:T(8,128)(2,1)}, u32[]{:S(2)}) copy-start(bf16[384,1536]{1,0:T(8,128)(2,1)} %all-gather.7.cloned.1.call-done) | copy-start | bytes 3538948
  129.0 6.8 %copy-start.40 = (bf16[8,256,1536]{2,1,0:T(8,128)(2,1)S(1)}, bf16[8,256,1536]{2,1,0:T(8,128)(2,1)}, u32[]{:S(2)}) copy-start(bf16[8,256,1536]{2,1,0:T(8,128)(2,1)} %get-tuple-element.205) | copy-start | bytes 18874372
  202.5 5.5 %copy-start.19 = (f32[8,384]{1,0:T(8,128)S(1)}, f32[8,384]{1,0:T(8,128)}, u32[]{:S(2)}) copy-start(f32[8,384]{1,0:T(8,128)} %get-tuple-element.194) | copy-start | bytes 36868
  202.5 5.5 %copy-start.23 = (f32[8,256]{1,0:T(8,128)S(1)}, f32[8,256]{1,0:T(8,128)}, u32[]{:S(2)}) copy-start(f32[8,256]{1,0:T(8,128)} %add_rsqrt_fusion) | copy-start | bytes 24580
  202.5 49.0 %reduce-scatter.8.cloned.1.call-start = ((), (), s32[]{:S(2)}) async-start(), calls=%async_computation.9 | async-start | bytes 1105920 | tf_op jit(solution)/shard_map/reduce_scatter | solution.py:189
  207.9 18.7 %copy-start.17 = (f32[8,384]{1,0:T(8,128)S(1)}, f32[8,384]{1,0:T(8,128)}, u32[]{:S(2)}) copy-start(f32[8,384]{1,0:T(8,128)} %get-tuple-element.192) | copy-start | bytes 36868
  207.9 71.8 %reduce-scatter.12.cloned.1.call-start = ((), (), s32[]{:S(2)}) async-start(), calls=%async_computation.11 | async-start | bytes 1474560 | tf_op jit(solution)/shard_map/reduce_scatter | solution.py:201
  215.7 92.5 %reduce-scatter.14.cloned.1.call-start = ((), (), s32[]{:S(2)}) async-start(), calls=%async_computation.12 | async-start | bytes 1474560 | tf_op jit(solution)/shard_map/reduce_scatter | solution.py:207
  234.3 6.3 %copy-start.25 = (f32[384]{0:T(512)S(1)}, f32[384]{0:T(512)}, u32[]{:S(2)}) copy-start(f32[384]{0:T(512)} %convert_element_type.177) | copy-start | bytes 4612
  234.3 105.9 %reduce-scatter.6.cloned.1.call-start = ((), (), s32[]{:S(2)}) async-start(), calls=%async_computation.8 | async-start | bytes 2211840 | tf_op jit(solution)/shard_map/reduce_scatter | solution.py:183
  234.4 6.3 %copy-start.4 = (f32[8,256,384]{2,1,0:T(8,128)S(1)}, f32[8,256,384]{2,1,0:T(8,128)}, u32[]{:S(2)}) copy-start(f32[8,256,384]{2,1,0:T(8,128)} %get-tuple-element.204) | copy-start | bytes 9437188
  234.4 6.3 %copy-start.5 = (f32[8,256,384]{2,1,0:T(8,128)S(1)}, f32[8,256,384]{2,1,0:T(8,128)}, u32[]{:S(2)}) copy-start(f32[8,256,384]{2,1,0:T(8,128)} %get-tuple-element.174) | copy-start | bytes 9437188
  245.9 99.3 %copy-start.32 = (bf16[384]{0:T(512)(128)(2,1)S(1)}, bf16[384]{0:T(512)(128)(2,1)}, u32[]{:S(2)}) copy-start(bf16[384]{0:T(512)(128)(2,1)} %get-tuple-element.172) | copy-start | bytes 2308
  245.9 99.3 %copy-start.33 = (bf16[384]{0:T(512)(128)(2,1)S(1)}, bf16[384]{0:T(512)(128)(2,1)}, u32[]{:S(2)}) copy-start(bf16[384]{0:T(512)(128)(2,1)} %get-tuple-element.191) | copy-start | bytes 2308
  245.9 99.3 %copy-start.34 = (bf16[1536]{0:T(1024)(128)(2,1)S(1)}, bf16[1536]{0:T(1024)(128)(2,1)}, u32[]{:S(2)}) copy-start(bf16[1536]{0:T(1024)(128)(2,1)} %get-tuple-element.208) | copy-start | bytes 9220
  245.9 135.1 %copy-start.6 = (bf16[384,2304]{1,0:T(8,128)(2,1)S(1)}, bf16[384,2304]{1,0:T(8,128)(2,1)}, u32[]{:S(2)}) copy-start(bf16[384,2304]{1,0:T(8,128)(2,1)} %all-gather.5.cloned.1.call-done) | copy-start | bytes 5308420
  245.9 184.3 %all-reduce.15.cloned.1.call-start = ((), (), s32[]{:S(2)}) async-start(), calls=%async_computation.13 | async-start | bytes 2654208 | tf_op jit(solution)/shard_map/psum | solution.py:215
  430.2 5.7 %copy-start.11 = (bf16[96,1152]{1,0:T(8,128)(2,1)S(1)}, bf16[96,1152]{1,0:T(8,128)(2,1)}, u32[]{:S(2)}) copy-start(bf16[96,1152]{1,0:T(8,128)(2,1)} %get-tuple-element.159) | copy-start | bytes 663556
  430.2 6.5 %copy-start.12 = (bf16[96,384]{1,0:T(8,128)(2,1)S(1)}, bf16[96,384]{1,0:T(8,128)(2,1)}, u32[]{:S(2)}) copy-start(bf16[96,384]{1,0:T(8,128)(2,1)} %get-tuple-element.160) | copy-start | bytes 221188
  (24 other events, 79.8 us)
Sparse Core Ops, SparseCore 0:
  9.6 23.7 all-gather.4
  34.9 18.7 all-gather.6
  55.3 17.2 all-gather.8
  202.6 21.8 reduce-scatter.9
  227.6 23.8 reduce-scatter.7
  254.0 25.7 reduce-scatter.11
  282.4 25.6 reduce-scatter.13
  310.8 29.3 reduce-scatter.5
  344.8 85.3 all-reduce.14
